TPU v7x, 32 devices: a whole 2x2x4 slice. The times are simulated.
32 devices in a mesh: dp: 8 (over y, x, core), tensor: 4 (over z).
Axes of the slice: x: 2, y: 2, z: 4, core: 2. Of those that a mesh axis runs over, the one named last changes fastest.
Arguments:
- tokens: bfloat16 [12288, 2048], P(('dp', 'tensor')), may hold values from -6 to 6
- norm_attn: bfloat16 [2048], P('dp'), may hold values from 0.099609375 to 1.8984375
- w_query: bfloat16 [2048, 2048], P('dp', 'tensor'), may hold values from -0.125 to 0.125
- w_key: bfloat16 [2048, 128], P('dp'), may hold values from -0.125 to 0.125
- w_value: bfloat16 [2048, 128], P('dp'), may hold values from -0.125 to 0.125
- w_out: bfloat16 [2048, 2048], P('tensor', 'dp'), may hold values from -0.75 to 0.75
- norm_ffn: bfloat16 [2048], P('dp'), may hold values from 0.099609375 to 1.8984375
- w_gate: bfloat16 [2048, 5632], P('dp', 'tensor'), may hold values from -0.125 to 0.125
- w_up: bfloat16 [2048, 5632], P('dp', 'tensor'), may hold values from -0.125 to 0.125
- w_down: bfloat16 [5632, 2048], P('tensor', 'dp'), may hold values from -0.078125 to 0.078125
- segment_ids: int32 [12288], P('dp'), may hold values from 0 to 103, as said below
- parents: int32 [104], replicated, may hold values from 0 to 95, as said below
- positions: int32 [12288], P('dp'), may hold values from 0 to 927, as said below
- d_out: bfloat16 [12288, 2048], P(('dp', 'tensor')), may hold values from -6 to 6
- d_keys: bfloat16 [12288, 128], P(('dp', 'tensor')), may hold values from -6 to 6
- d_values: bfloat16 [12288, 128], P(('dp', 'tensor')), may hold values from -6 to 6
Outputs:
- out: bfloat16 [12288, 2048], P(('dp', 'tensor'))
- keys: bfloat16 [12288, 128], P('dp')
- values: bfloat16 [12288, 128], P('dp')
- d_x: float32 [12288, 2048], P(('dp', 'tensor'))
- g_norm_attn: float32 [2048], P('dp')
- g_query: float32 [2048, 2048], P('dp', 'tensor')
- g_key: float32 [2048, 128], P('dp')
- g_value: float32 [2048, 128], P('dp')
- g_out: float32 [2048, 2048], P('tensor', 'dp')
- g_norm_ffn: float32 [2048], P('dp')
- g_gate: float32 [2048, 5632], P('dp', 'tensor')
- g_up: float32 [2048, 5632], P('dp', 'tensor')
- g_down: float32 [5632, 2048], P('tensor', 'dp')
Inputs may be any that keep to these rules, and one draw needn't show every extreme that they name: `segment_ids`: tree t holds tokens t * 1536 to (t + 1) * 1536 - 1 and segments 13 t to 13 t + 12 in this order: a trunk of 768 tokens, four branches of 64 tokens, eight leaves whose two of each branch have lengths summing to 128, each leaf 64 // 2 tokens or more; ids never fall. `parents`: A trunk is its own parent, a branch's parent is its tree's trunk, a leaf's parent is a branch of its tree, and each branch is the parent of exactly two leaves. `positions`: counts up by one within a segment from 0 at a trunk's first token, from 768 at a branch's first token and from 832 at a leaf's first token.
All inputs are finite; a program needn't handle non-finite values.
Results may differ from a plain program's by a relative error of at most 0.022.
Values may be sent and summed in bfloat16 or wider, within the bound.
No kernel may reach another device: no remote copies, remote signals or barrier semaphores. Data moves between devices by JAX's collectives and lax.ppermute only.
A program may use at most 256 MiB of HBM per device.

v0:
```python
import jax
import jax.numpy as jnp
from jax import lax
from jax.sharding import PartitionSpec as P

HD = 128
QBLOCK = 512
norm_eps = 1e-05


def lookup(ids, table):
    hits = ids[:, None] == jnp.arange(table.shape[0], dtype=jnp.int32)[None, :]
    return jnp.sum(jnp.where(hits, table[None, :], 0), axis=1)


def path_mask(segment_block, first_block, second_block, place_block, segment, place):
    linked = (
        (segment[None, :] == segment_block[:, None])
        | (segment[None, :] == first_block[:, None])
        | (segment[None, :] == second_block[:, None])
    )
    return linked & (place[None, :] <= place_block[:, None])


def norm_back(value, scale, gain, grad):
    weighted = grad * gain
    return scale * weighted - value * (scale * scale * scale) * jnp.mean(
        weighted * value, axis=-1, keepdims=True
    )


def contract_rows(left, right):
    return lax.dot_general(
        left, right, (((0,), (0,)), ((), ())), preferred_element_type=jnp.float32
    )


def contract_cols(left, right):
    return lax.dot_general(
        left, right, (((1,), (1,)), ((), ())), preferred_element_type=jnp.float32
    )


def on_device(
    tokens,
    norm_attn,
    w_query,
    w_key,
    w_value,
    w_out,
    norm_ffn,
    w_gate,
    w_up,
    w_down,
    segment_ids,
    parents,
    positions,
    d_out,
    d_keys,
    d_values,
):
    score_scale = HD ** (-0.5)
    attn_gain, query_w, key_w, value_w, out_w = (
        lax.all_gather(norm_attn, "dp", axis=0, tiled=True),
        lax.all_gather(w_query, "dp", axis=0, tiled=True),
        lax.all_gather(w_key, "dp", axis=0, tiled=True),
        lax.all_gather(w_value, "dp", axis=0, tiled=True),
        lax.all_gather(w_out, "dp", axis=1, tiled=True),
    )
    ffn_gain, gate_w, up_w, down_w = (
        lax.all_gather(norm_ffn, "dp", axis=0, tiled=True),
        lax.all_gather(w_gate, "dp", axis=0, tiled=True),
        lax.all_gather(w_up, "dp", axis=0, tiled=True),
        lax.all_gather(w_down, "dp", axis=1, tiled=True),
    )
    attn_gain = attn_gain.astype(jnp.float32)
    ffn_gain = ffn_gain.astype(jnp.float32)
    residual = tokens.astype(jnp.float32)
    attn_scale = lax.rsqrt(jnp.mean(residual * residual, axis=-1, keepdims=True) + norm_eps)
    normed_own = (residual * attn_scale * attn_gain).astype(jnp.bfloat16)
    normed = lax.all_gather(normed_own, "tensor", axis=0, tiled=True)
    query = jnp.dot(normed, query_w, preferred_element_type=jnp.float32).astype(jnp.bfloat16)
    keys = jnp.dot(normed, key_w, preferred_element_type=jnp.float32).astype(jnp.bfloat16)
    values = jnp.dot(normed, value_w, preferred_element_type=jnp.float32).astype(jnp.bfloat16)
    total = normed.shape[0]
    blocks = total // QBLOCK
    heads = query.shape[1] // HD
    first_up = lookup(segment_ids, parents)
    second_up = lookup(first_up, parents)
    query_blocks = query.reshape(blocks, QBLOCK, heads, HD)
    id_blocks = (
        segment_ids.reshape(blocks, QBLOCK),
        first_up.reshape(blocks, QBLOCK),
        second_up.reshape(blocks, QBLOCK),
        positions.reshape(blocks, QBLOCK),
    )

    def attend(operand):
        query_block, segment_block, first_block, second_block, place_block = operand
        mask = path_mask(
            segment_block, first_block, second_block, place_block, segment_ids, positions
        )
        scores = (
            jnp.einsum("qhd,kd->hqk", query_block, keys, preferred_element_type=jnp.float32)
            * score_scale
        )
        scores = jnp.where(mask[None], scores, -1e30)
        peak = jnp.max(scores, axis=-1, keepdims=True)
        raised = jnp.exp(scores - peak)
        sums = jnp.sum(raised, axis=-1, keepdims=True)
        shares = (raised / sums).astype(jnp.bfloat16)
        mixed_block = jnp.einsum(
            "hqk,kd->qhd", shares, values, preferred_element_type=jnp.float32
        ).astype(jnp.bfloat16)
        return (mixed_block.reshape(QBLOCK, heads * HD), (peak + jnp.log(sums))[..., 0])

    mixed, log_totals = lax.map(attend, (query_blocks,) + id_blocks)
    mixed = mixed.reshape(total, heads * HD)
    attn_part = lax.psum_scatter(
        jnp.dot(mixed, out_w, preferred_element_type=jnp.float32),
        "tensor",
        scatter_dimension=0,
        tiled=True,
    )
    after_attn = residual + attn_part
    ffn_scale = lax.rsqrt(jnp.mean(after_attn * after_attn, axis=-1, keepdims=True) + norm_eps)
    ffn_own = (after_attn * ffn_scale * ffn_gain).astype(jnp.bfloat16)
    ffn_normed = lax.all_gather(ffn_own, "tensor", axis=0, tiled=True)
    gate = jnp.dot(ffn_normed, gate_w, preferred_element_type=jnp.float32)
    upward = jnp.dot(ffn_normed, up_w, preferred_element_type=jnp.float32)
    sigma = jax.nn.sigmoid(gate)
    hidden = (gate * sigma * upward).astype(jnp.bfloat16)
    ffn_part = lax.psum_scatter(
        jnp.dot(hidden, down_w, preferred_element_type=jnp.float32).astype(jnp.bfloat16),
        "tensor",
        scatter_dimension=0,
        tiled=True,
    ).astype(jnp.float32)
    output = (after_attn + ffn_part).astype(jnp.bfloat16)
    grad_full = lax.all_gather(d_out, "tensor", axis=0, tiled=True)
    down_grad = contract_rows(hidden, grad_full)
    hidden_grad = contract_cols(grad_full, down_w)
    gate_grad = (hidden_grad * upward * sigma * (1.0 + gate * (1.0 - sigma))).astype(jnp.bfloat16)
    up_grad = (hidden_grad * gate * sigma).astype(jnp.bfloat16)
    gate_w_grad = contract_rows(ffn_normed, gate_grad)
    up_w_grad = contract_rows(ffn_normed, up_grad)
    ffn_normed_grad = lax.psum_scatter(
        contract_cols(gate_grad, gate_w) + contract_cols(up_grad, up_w),
        "tensor",
        scatter_dimension=0,
        tiled=True,
    )
    after_grad = d_out.astype(jnp.float32) + norm_back(
        after_attn, ffn_scale, ffn_gain, ffn_normed_grad
    )
    ffn_gain_term = jnp.sum(ffn_normed_grad * after_attn * ffn_scale, axis=0)
    branch_full = lax.all_gather(after_grad.astype(jnp.bfloat16), "tensor", axis=0, tiled=True)
    out_w_grad = contract_rows(mixed, branch_full)
    mixed_grad = contract_cols(branch_full, out_w).astype(jnp.bfloat16)
    mixed_grad_blocks = mixed_grad.reshape(blocks, QBLOCK, heads, HD)

    def attend_back(carry, operand):
        key_acc, value_acc = carry
        (
            query_block,
            grad_block,
            log_block,
            segment_block,
            first_block,
            second_block,
            place_block,
        ) = operand
        mask = path_mask(
            segment_block, first_block, second_block, place_block, segment_ids, positions
        )
        scores = (
            jnp.einsum("qhd,kd->hqk", query_block, keys, preferred_element_type=jnp.float32)
            * score_scale
        )
        scores = jnp.where(mask[None], scores, -1e30)
        shares = jnp.exp(scores - log_block[:, :, None])
        low_shares = shares.astype(jnp.bfloat16)
        share_grad = jnp.einsum(
            "qhd,kd->hqk", grad_block, values, preferred_element_type=jnp.float32
        )
        value_acc = value_acc + jnp.einsum(
            "hqk,qhd->kd", low_shares, grad_block, preferred_element_type=jnp.float32
        )
        inner = jnp.sum(shares * share_grad, axis=-1, keepdims=True)
        score_grad = (shares * (share_grad - inner)).astype(jnp.bfloat16)
        query_grad_block = (
            score_scale
            * jnp.einsum("hqk,kd->qhd", score_grad, keys, preferred_element_type=jnp.float32)
        ).astype(jnp.bfloat16)
        key_acc = key_acc + score_scale * jnp.einsum(
            "hqk,qhd->kd", score_grad, query_block, preferred_element_type=jnp.float32
        )
        return ((key_acc, value_acc), query_grad_block.reshape(QBLOCK, heads * HD))

    empty = jnp.zeros((total, HD), jnp.float32)
    (key_acc, value_acc), query_grad = lax.scan(
        attend_back, (empty, empty), (query_blocks, mixed_grad_blocks, log_totals) + id_blocks
    )
    query_grad = query_grad.reshape(total, heads * HD)
    query_w_grad = contract_rows(normed, query_grad)
    normed_part = contract_cols(query_grad, query_w)
    normed_sum, key_sum, value_sum = (
        lax.psum_scatter(
            normed_part.astype(jnp.bfloat16), "tensor", scatter_dimension=0, tiled=True
        ).astype(jnp.float32),
        lax.psum_scatter(
            key_acc.astype(jnp.bfloat16), "tensor", scatter_dimension=0, tiled=True
        ).astype(jnp.float32),
        lax.psum_scatter(
            value_acc.astype(jnp.bfloat16), "tensor", scatter_dimension=0, tiled=True
        ).astype(jnp.float32),
    )
    key_grad = (key_sum + d_keys.astype(jnp.float32)).astype(jnp.bfloat16)
    value_grad = (value_sum + d_values.astype(jnp.float32)).astype(jnp.bfloat16)
    normed_grad = normed_sum + contract_cols(key_grad, key_w) + contract_cols(value_grad, value_w)
    key_w_term = contract_rows(normed_own, key_grad)
    value_w_term = contract_rows(normed_own, value_grad)
    input_grad = after_grad + norm_back(residual, attn_scale, attn_gain, normed_grad)
    attn_gain_term = jnp.sum(normed_grad * residual * attn_scale, axis=0)
    key_w_grad, value_w_grad, attn_gain_grad, ffn_gain_grad = (
        lax.psum(key_w_term.astype(jnp.bfloat16), "tensor").astype(jnp.float32),
        lax.psum(value_w_term.astype(jnp.bfloat16), "tensor").astype(jnp.float32),
        lax.psum(attn_gain_term.astype(jnp.bfloat16), "tensor").astype(jnp.float32),
        lax.psum(ffn_gain_term.astype(jnp.bfloat16), "tensor").astype(jnp.float32),
    )
    (
        attn_gain_part,
        query_part,
        key_part,
        value_part,
        out_part,
        ffn_gain_part,
        gate_part,
        up_part,
        down_part,
    ) = (
        lax.psum_scatter(
            attn_gain_grad.astype(jnp.bfloat16), "dp", scatter_dimension=0, tiled=True
        ).astype(jnp.float32),
        lax.psum_scatter(
            query_w_grad.astype(jnp.bfloat16), "dp", scatter_dimension=0, tiled=True
        ).astype(jnp.float32),
        lax.psum_scatter(
            key_w_grad.astype(jnp.bfloat16), "dp", scatter_dimension=0, tiled=True
        ).astype(jnp.float32),
        lax.psum_scatter(
            value_w_grad.astype(jnp.bfloat16), "dp", scatter_dimension=0, tiled=True
        ).astype(jnp.float32),
        lax.psum_scatter(
            out_w_grad.astype(jnp.bfloat16), "dp", scatter_dimension=1, tiled=True
        ).astype(jnp.float32),
        lax.psum_scatter(
            ffn_gain_grad.astype(jnp.bfloat16), "dp", scatter_dimension=0, tiled=True
        ).astype(jnp.float32),
        lax.psum_scatter(
            gate_w_grad.astype(jnp.bfloat16), "dp", scatter_dimension=0, tiled=True
        ).astype(jnp.float32),
        lax.psum_scatter(
            up_w_grad.astype(jnp.bfloat16), "dp", scatter_dimension=0, tiled=True
        ).astype(jnp.float32),
        lax.psum_scatter(
            down_grad.astype(jnp.bfloat16), "dp", scatter_dimension=1, tiled=True
        ).astype(jnp.float32),
    )
    return (
        output,
        keys,
        values,
        input_grad,
        attn_gain_part,
        query_part,
        key_part,
        value_part,
        out_part,
        ffn_gain_part,
        gate_part,
        up_part,
        down_part,
    )


def solution(mesh):
    in_specs = (
        P(("dp", "tensor"), None),
        P("dp"),
        P("dp", "tensor"),
        P("dp", None),
        P("dp", None),
        P("tensor", "dp"),
        P("dp"),
        P("dp", "tensor"),
        P("dp", "tensor"),
        P("tensor", "dp"),
        P("dp"),
        P(),
        P("dp"),
        P(("dp", "tensor"), None),
        P(("dp", "tensor"), None),
        P(("dp", "tensor"), None),
    )
    out_specs = (
        P(("dp", "tensor"), None),
        P("dp", None),
        P("dp", None),
        P(("dp", "tensor"), None),
        P("dp"),
        P("dp", "tensor"),
        P("dp", None),
        P("dp", None),
        P("tensor", "dp"),
        P("dp"),
        P("dp", "tensor"),
        P("dp", "tensor"),
        P("tensor", "dp"),
    )
    return jax.shard_map(
        on_device, mesh=mesh, in_specs=in_specs, out_specs=out_specs, check_vma=False
    )
```

profile of v0, /device:TPU:0, one launch (start us, length us, event | category | flops | bytes accessed | tf_op | source)
XLA Modules:
  0.0 1988.7 jit_solution(13247573112457298185)
XLA Ops:
  10.4 10.3 all-gather
  26.3 9.8 all_gather.42
  36.1 8.9 all_gather.43
  45.0 95.1 %all-gather.12.cloned.1.call-done = bf16[1536,2048]{1,0:T(8,128)(2,1)} async-done(((bf16[384,2048]{1,0:T(8,128)(2,1)}), bf16[1536,2048]{1,0:T(8,128)(2,1)}) %all-gather.12.cloned.1.call-update) | async-done | bytes 6291472 | tf_op jit(solution)/shard_map/all_gather | solution.py:81
  144.9 23.3 %all-gather.14.cloned.1.call-done = bf16[2048,512]{1,0:T(8,128)(2,1)} async-done(((bf16[256,512]{1,0:T(8,128)(2,1)}), bf16[2048,512]{1,0:T(8,128)(2,1)}) %all-gather.14.cloned.1.call-update) | async-done | bytes 2097168 | tf_op jit(solution)/shard_map/all_gather | solution.py:65
  168.2 8.0 convolution_convert_fusion.8
  184.9 40.4 %while.27 = (s32[]{:T(128)}, bf16[3,512,512]{2,1,0:T(8,128)(2,1)S(1)}, f32[3,4,512]{2,1,0:T(4,128)S(1)}, s32[1536]{0:T(1024)S(1)}, s32[3,512]{1,0:T(4,128)S(1)},...) while((s32[]{:T(128)}, ...), condition=%wide.region_6.7_spmd, body=%wide.region_3.6_spmd.sunk | while | flops 1654126592 | bytes 44929176 | solution.py:117
  225.4 8.6 fusion.48
  234.7 8.8 all-gather.1
  243.5 202.5 %reduce-scatter.14.cloned.1.call-done = f32[384,2048]{1,0:T(8,128)} async-done(((f32[1536,2048]{1,0:T(8,128)}), f32[384,2048]{1,0:T(8,128)}) %reduce-scatter.14.cloned.1.call-update) | async-done | bytes 3145744 | tf_op jit(solution)/shard_map/reduce_scatter | solution.py:119
  452.7 39.5 %all-gather.22.cloned.1.call-done = bf16[2048,1408]{1,0:T(8,128)(2,1)} async-done(((bf16[256,1408]{1,0:T(8,128)(2,1)}), bf16[2048,1408]{1,0:T(8,128)(2,1)}) %all-gather.22.cloned.1.call-update) | async-done | bytes 5767184 | tf_op jit(solution)/shard_map/all_gather | solution.py:73
  492.1 117.4 %all-gather.18.cloned.1.call-done = bf16[1536,2048]{1,0:T(8,128)(2,1)} async-done(((bf16[384,2048]{1,0:T(8,128)(2,1)}), bf16[1536,2048]{1,0:T(8,128)(2,1)}) %all-gather.18.cloned.1.call-update) | async-done | bytes 6291472 | tf_op jit(solution)/shard_map/all_gather | solution.py:128
  609.5 15.3 fusion.50
  624.8 28.2 %all-gather.20.cloned.1.call-done = bf16[2048,1408]{1,0:T(8,128)(2,1)} async-done(((bf16[256,1408]{1,0:T(8,128)(2,1)}), bf16[2048,1408]{1,0:T(8,128)(2,1)}) %all-gather.20.cloned.1.call-update) | async-done | bytes 5767184 | tf_op jit(solution)/shard_map/all_gather | solution.py:72
  653.0 15.1 fusion.49
  668.1 101.8 %all-gather.26.cloned.1.call-done = bf16[1536,2048]{1,0:T(8,128)(2,1)} async-done(((bf16[384,2048]{1,0:T(8,128)(2,1)}), bf16[1536,2048]{1,0:T(8,128)(2,1)}) %all-gather.26.cloned.1.call-update) | async-done | bytes 6291472 | tf_op jit(solution)/shard_map/all_gather | solution.py:140
  769.9 44.5 %all-gather.24.cloned.1.call-done = bf16[1408,2048]{1,0:T(8,128)(2,1)} async-done(((bf16[1408,256]{1,0:T(8,128)(2,1)}), bf16[1408,2048]{1,0:T(8,128)(2,1)}) %all-gather.24.cloned.1.call-update) | async-done | bytes 5767184 | tf_op jit(solution)/shard_map/all_gather | solution.py:74
  814.4 22.9 %multiply_convert_fusion = (bf16[1536,1408]{1,0:T(8,128)(2,1)}, bf16[1536,1408]{1,0:T(8,128)(2,1)}, bf16[1536,1408]{1,0:T(8,128)(2,1)}) fusion(f32[1536,1408]{1,0:T(8,128)} %fusion.49, f32[1536,1408]{1,0:T(8,128)} %fusion.50, bf16[1536,2048]{1,0:T(8,128)(2,1)} %all-gather.26.cloned.1.call-done, bf16[1408,2048]{1,0:T(8,128)(2,1)} %all-gather.24.cloned.1.call-done), kind=kOutput, calls=%fused_computation.58 | convolution fusion | flops 8892973056 | bytes 42336256 | tf_op jit(solution)/shard_map/dot_general | solution.py:39
  837.4 16.6 fusion.51
  854.0 16.4 convolution_add_fusion
  870.5 15.0 convolution_convert_fusion.4
  885.6 196.9 %reduce-scatter.18.cloned.1.call-done = f32[384,2048]{1,0:T(8,128)} async-done(((f32[1536,2048]{1,0:T(8,128)}), f32[384,2048]{1,0:T(8,128)}) %reduce-scatter.18.cloned.1.call-update) | async-done | bytes 3145744 | tf_op jit(solution)/shard_map/reduce_scatter | solution.py:147
  1085.7 110.9 %reduce-scatter.16.cloned.1.call-done = bf16[384,2048]{1,0:T(8,128)(2,1)} async-done(((bf16[1536,2048]{1,0:T(8,128)(2,1)}), bf16[384,2048]{1,0:T(8,128)(2,1)}) %reduce-scatter.16.cloned.1.call-update) | async-done | bytes 1572880 | tf_op jit(solution)/shard_map/reduce_scatter | solution.py:133
  1196.6 6.7 fusion.47
  1205.3 114.1 %all-gather.28.cloned.1.call-done = bf16[1536,2048]{1,0:T(8,128)(2,1)} async-done(((bf16[384,2048]{1,0:T(8,128)(2,1)}), bf16[1536,2048]{1,0:T(8,128)(2,1)}) %all-gather.28.cloned.1.call-update) | async-done | bytes 6291472 | tf_op jit(solution)/shard_map/all_gather | solution.py:157
  1319.4 6.9 convolution_convert_fusion.7
  1329.6 71.5 %while.28 = (s32[]{:T(128)}, f32[1536,128]{1,0:T(8,128)}, f32[1536,128]{1,0:T(8,128)S(1)}, bf16[3,512,512]{2,1,0:T(8,128)(2,1)}, s32[1536]{0:T(1024)S(1)}, /*ind...) while((s32[]{:T(128)}, f32[1536,128]{1,0:T(8,128)}, ...), condition=%wide.region_14.15_spmd.clone, body=%wide.region_12.14_spmd.clone.sunk | while | flops 4061853696 | bytes 139145552 | solution.py:201
  1334.9 5.6 fusion.117
  1358.8 5.6 fusion.117
  1382.6 5.6 fusion.117
  1404.3 17.9 reduce-scatter.22.cloned.1.call-done
  1425.1 18.7 reduce-scatter.24.cloned.1.call-done
  1446.2 14.3 convolution_convert_fusion
  1460.6 15.0 convolution_convert_fusion.1
  1475.9 15.0 convolution_convert_fusion.2
  1491.0 26.8 %reduce-scatter.38.cloned.1.call-done = bf16[256,128]{1,0:T(8,128)(2,1)} async-done(((bf16[2048,128]{1,0:T(8,128)(2,1)}), bf16[256,128]{1,0:T(8,128)(2,1)}) %reduce-scatter.38.cloned.1.call-update) | async-done | bytes 65552 | tf_op jit(solution)/shard_map/reduce_scatter | solution.py:251
  1517.9 7.8 convolution_convert_fusion.6
  1525.8 7.9 convolution_convert_fusion.5
  1534.0 7.2 convolution_convert_fusion.3
  1543.1 37.1 %reduce-scatter.34.cloned.1.call-done = bf16[1408,256]{1,0:T(8,128)(2,1)} async-done(((bf16[1408,2048]{1,0:T(8,128)(2,1)}), bf16[1408,256]{1,0:T(8,128)(2,1)}) %reduce-scatter.34.cloned.1.call-update) | async-done | bytes 720912 | tf_op jit(solution)/shard_map/reduce_scatter | solution.py:266
  1582.5 60.4 %reduce-scatter.32.cloned.1.call-done = bf16[256,1408]{1,0:T(8,128)(2,1)} async-done(((bf16[2048,1408]{1,0:T(8,128)(2,1)}), bf16[256,1408]{1,0:T(8,128)(2,1)}) %reduce-scatter.32.cloned.1.call-update) | async-done | bytes 720912 | tf_op jit(solution)/shard_map/reduce_scatter | solution.py:263
  1645.3 60.2 %reduce-scatter.30.cloned.1.call-done = bf16[256,1408]{1,0:T(8,128)(2,1)} async-done(((bf16[2048,1408]{1,0:T(8,128)(2,1)}), bf16[256,1408]{1,0:T(8,128)(2,1)}) %reduce-scatter.30.cloned.1.call-update) | async-done | bytes 720912 | tf_op jit(solution)/shard_map/reduce_scatter | solution.py:260
  1710.0 32.3 %all-reduce.7.cloned.1.call-done = (bf16[256,128]{1,0:T(8,128)(2,1)}, bf16[256,128]{1,0:T(8,128)(2,1)}) async-done(((bf16[256,128]{1,0:T(8,128)(2,1)}, bf16[256,128]{1,0:T(8,128)(2,1)}), (bf16[256,128]{1,0:T(8,128)(2,1)}, bf16[256,128]{1,0:T(8,128)(2,1)})) %all-reduce.7.cloned.1.call-update) | async-done | bytes 131088 | tf_op jit(solution)/shard_map/psum | solution.py:226
  1745.3 41.2 %reduce-scatter.26.cloned.1.call-done = bf16[256,512]{1,0:T(8,128)(2,1)} async-done(((bf16[2048,512]{1,0:T(8,128)(2,1)}), bf16[256,512]{1,0:T(8,128)(2,1)}) %reduce-scatter.26.cloned.1.call-update) | async-done | bytes 262160 | tf_op jit(solution)/shard_map/reduce_scatter | solution.py:245
  1788.4 43.1 %reduce-scatter.28.cloned.1.call-done = bf16[512,256]{1,0:T(8,128)(2,1)} async-done(((bf16[512,2048]{1,0:T(8,128)(2,1)}), bf16[512,256]{1,0:T(8,128)(2,1)}) %reduce-scatter.28.cloned.1.call-update) | async-done | bytes 262160 | tf_op jit(solution)/shard_map/reduce_scatter | solution.py:254
  1833.3 111.3 %reduce-scatter.20.cloned.1.call-done = bf16[384,2048]{1,0:T(8,128)(2,1)} async-done(((bf16[1536,2048]{1,0:T(8,128)(2,1)}), bf16[384,2048]{1,0:T(8,128)(2,1)}) %reduce-scatter.20.cloned.1.call-update) | async-done | bytes 1572880 | tf_op jit(solution)/shard_map/reduce_scatter | solution.py:208
  1949.9 14.0 all-reduce.2
  1964.0 11.1 all-reduce.3
  (243 shorter events, 171.1 us)
Async XLA Ops:
  7.2 18.7 copy-start.15
  7.2 18.7 copy-start.29
  7.2 19.1 copy-start.16
  7.2 19.1 copy-start.23
  7.2 28.9 %copy-start.24 = (bf16[256,128]{1,0:T(8,128)(2,1)S(1)}, bf16[256,128]{1,0:T(8,128)(2,1)}, u32[]{:S(2)}) copy-start(bf16[256,128]{1,0:T(8,128)(2,1)} %param.24) | copy-start | bytes 196612
  7.2 132.9 %all-gather.12.cloned.1.call-start = ((), (), s32[]{:S(2)}) async-start(), calls=%async_computation.13 | async-start | bytes 7864320 | tf_op jit(solution)/shard_map/all_gather | solution.py:81
  10.4 134.3 %copy-start.25 = (f32[384]{0:T(512)}, f32[384]{0:T(512)S(1)}, u32[]{:S(2)}) copy-start(f32[384]{0:T(512)S(1)} %get-tuple-element.401) | copy-start | bytes 4612
  24.3 143.9 %all-gather.14.cloned.1.call-start = ((), (), s32[]{:S(2)}) async-start(), calls=%async_computation.14 | async-start | bytes 2359296 | tf_op jit(solution)/shard_map/all_gather | solution.py:65
  25.1 200.3 %all-gather.16.cloned.1.call-start = ((), (), s32[]{:S(2)}) async-start(), calls=%async_computation.15 | async-start | bytes 2359296 | tf_op jit(solution)/shard_map/all_gather | solution.py:68
  25.8 420.2 %reduce-scatter.14.cloned.1.call-start = ((), (), s32[]{:S(2)}) async-start(), calls=%async_computation.16 | async-start | bytes 15728640 | tf_op jit(solution)/shard_map/reduce_scatter | solution.py:119
  36.1 144.1 %copy-start.10 = (bf16[2048,128]{1,0:T(8,128)(2,1)}, bf16[2048,128]{1,0:T(8,128)(2,1)S(1)}, u32[]{:S(2)}) copy-start(bf16[2048,128]{1,0:T(8,128)(2,1)S(1)} %all_gather.42) | copy-start | bytes 1572868
  45.0 123.2 %copy-start.8 = (bf16[2048,128]{1,0:T(8,128)(2,1)}, bf16[2048,128]{1,0:T(8,128)(2,1)S(1)}, u32[]{:S(2)}) copy-start(bf16[2048,128]{1,0:T(8,128)(2,1)S(1)} %all_gather.43) | copy-start | bytes 1572868
  144.7 31.4 %copy-start.5 = (bf16[1536,128]{1,0:T(8,128)(2,1)}, bf16[1536,128]{1,0:T(8,128)(2,1)S(1)}, u32[]{:S(2)}) copy-start(bf16[1536,128]{1,0:T(8,128)(2,1)S(1)} %convolution_convert_fusion.11) | copy-start | bytes 1179652
  225.4 8.6 copy-start.6
  225.4 8.6 copy-start.13
  234.0 258.1 %all-gather.22.cloned.1.call-start = ((), (), s32[]{:S(2)}) async-start(), calls=%async_computation.19 | async-start | bytes 6488064 | tf_op jit(solution)/shard_map/all_gather | solution.py:73
  234.6 374.9 %all-gather.18.cloned.1.call-start = ((), (), s32[]{:S(2)}) async-start(), calls=%async_computation.17 | async-start | bytes 7864320 | tf_op jit(solution)/shard_map/all_gather | solution.py:128
  450.4 202.6 %all-gather.20.cloned.1.call-start = ((), (), s32[]{:S(2)}) async-start(), calls=%async_computation.18 | async-start | bytes 6488064 | tf_op jit(solution)/shard_map/all_gather | solution.py:72
  451.1 318.8 %all-gather.26.cloned.1.call-start = ((), (), s32[]{:S(2)}) async-start(), calls=%async_computation.22 | async-start | bytes 7864320 | tf_op jit(solution)/shard_map/all_gather | solution.py:140
  451.9 362.6 %all-gather.24.cloned.1.call-start = ((), (), s32[]{:S(2)}) async-start(), calls=%async_computation.20 | async-start | bytes 6488064 | tf_op jit(solution)/shard_map/all_gather | solution.py:74
  452.6 629.9 %reduce-scatter.18.cloned.1.call-start = ((), (), s32[]{:S(2)}) async-start(), calls=%async_computation.23 | async-start | bytes 15728640 | tf_op jit(solution)/shard_map/reduce_scatter | solution.py:147
  837.4 16.6 copy-start.32
  870.5 326.1 %reduce-scatter.16.cloned.1.call-start = ((), (), s32[]{:S(2)}) async-start(), calls=%async_computation.21 | async-start | bytes 7864320 | tf_op jit(solution)/shard_map/reduce_scatter | solution.py:133
  885.6 433.8 %all-gather.28.cloned.1.call-start = ((), (), s32[]{:S(2)}) async-start(), calls=%async_computation.24 | async-start | bytes 7864320 | tf_op jit(solution)/shard_map/all_gather | solution.py:157
  1203.3 218.8 %reduce-scatter.22.cloned.1.call-start = ((), (), s32[]{:S(2)}) async-start(), calls=%async_computation.26 | async-start | bytes 491520 | tf_op jit(solution)/shard_map/reduce_scatter | solution.py:211
  1401.1 42.7 %copy-start.4 = (bf16[384,2048]{1,0:T(8,128)(2,1)S(1)}, bf16[384,2048]{1,0:T(8,128)(2,1)}, u32[]{:S(2)}) copy-start(bf16[384,2048]{1,0:T(8,128)(2,1)} %fusion.39) | copy-start | bytes 4718596
  1401.1 42.7 %copy-start.17 = (bf16[384,128]{1,0:T(8,128)(2,1)S(1)}, bf16[384,128]{1,0:T(8,128)(2,1)}, u32[]{:S(2)}) copy-start(bf16[384,128]{1,0:T(8,128)(2,1)} %param.35) | copy-start | bytes 294916
  1403.2 40.7 %reduce-scatter.24.cloned.1.call-start = ((), (), s32[]{:S(2)}) async-start(), calls=%async_computation.27 | async-start | bytes 491520 | tf_op jit(solution)/shard_map/reduce_scatter | solution.py:214
  1404.0 87.0 %reduce-scatter.36.cloned.1.call-start = ((), (), s32[]{:S(2)}) async-start(), calls=%async_computation.33 | async-start | bytes 589824 | tf_op jit(solution)/shard_map/reduce_scatter | solution.py:248
  1425.1 92.8 %reduce-scatter.38.cloned.1.call-start = ((), (), s32[]{:S(2)}) async-start(), calls=%async_computation.34 | async-start | bytes 589824 | tf_op jit(solution)/shard_map/reduce_scatter | solution.py:251
  1446.2 134.0 %reduce-scatter.34.cloned.1.call-start = ((), (), s32[]{:S(2)}) async-start(), calls=%async_computation.32 | async-start | bytes 6488064 | tf_op jit(solution)/shard_map/reduce_scatter | solution.py:266
  1460.5 182.4 %reduce-scatter.32.cloned.1.call-start = ((), (), s32[]{:S(2)}) async-start(), calls=%async_computation.31 | async-start | bytes 6488064 | tf_op jit(solution)/shard_map/reduce_scatter | solution.py:263
  1475.6 229.8 %reduce-scatter.30.cloned.1.call-start = ((), (), s32[]{:S(2)}) async-start(), calls=%async_computation.30 | async-start | bytes 6488064 | tf_op jit(solution)/shard_map/reduce_scatter | solution.py:260
  1490.9 27.0 %copy-start.12 = (bf16[3,512,512]{2,1,0:T(8,128)(2,1)S(1)}, bf16[3,512,512]{2,1,0:T(8,128)(2,1)}, u32[]{:S(2)}) copy-start(bf16[3,512,512]{2,1,0:T(8,128)(2,1)} %get-tuple-element.157) | copy-start | bytes 4718596
  1490.9 251.4 %all-reduce.7.cloned.1.call-start = ((), (), s32[]{:S(2)}) async-start(), calls=%async_computation.35 | async-start | bytes 262144 | tf_op jit(solution)/shard_map/psum | solution.py:226
  1517.8 268.7 %reduce-scatter.26.cloned.1.call-start = ((), (), s32[]{:S(2)}) async-start(), calls=%async_computation.28 | async-start | bytes 2359296 | tf_op jit(solution)/shard_map/reduce_scatter | solution.py:245
  1525.7 305.8 %reduce-scatter.28.cloned.1.call-start = ((), (), s32[]{:S(2)}) async-start(), calls=%async_computation.29 | async-start | bytes 2359296 | tf_op jit(solution)/shard_map/reduce_scatter | solution.py:254
  1533.7 410.9 %reduce-scatter.20.cloned.1.call-start = ((), (), s32[]{:S(2)}) async-start(), calls=%async_computation.25 | async-start | bytes 7864320 | tf_op jit(solution)/shard_map/reduce_scatter | solution.py:208
  1541.2 166.5 %copy-start.11 = (bf16[2048,128]{1,0:T(8,128)(2,1)S(1)}, bf16[2048,128]{1,0:T(8,128)(2,1)}, u32[]{:S(2)}) copy-start(bf16[2048,128]{1,0:T(8,128)(2,1)} %copy-done.10) | copy-start | bytes 1572868
  1541.2 166.5 %copy-start.19 = (bf16[384,128]{1,0:T(8,128)(2,1)S(1)}, bf16[384,128]{1,0:T(8,128)(2,1)}, u32[]{:S(2)}) copy-start(bf16[384,128]{1,0:T(8,128)(2,1)} %param.34) | copy-start | bytes 294916
  1541.3 166.5 %copy-start.20 = (bf16[384,128]{1,0:T(8,128)(2,1)S(1)}, bf16[384,128]{1,0:T(8,128)(2,1)}, u32[]{:S(2)}) copy-start(bf16[384,128]{1,0:T(8,128)(2,1)} %reduce-scatter.22.cloned.1.call-done) | copy-start | bytes 294916
  1645.2 299.4 %copy-start.1 = (bf16[384,2048]{1,0:T(8,128)(2,1)S(1)}, bf16[384,2048]{1,0:T(8,128)(2,1)}, u32[]{:S(2)}) copy-start(bf16[384,2048]{1,0:T(8,128)(2,1)} %param.20) | copy-start | bytes 4718596
  1645.2 299.4 %copy-start.9 = (bf16[2048,128]{1,0:T(8,128)(2,1)S(1)}, bf16[2048,128]{1,0:T(8,128)(2,1)}, u32[]{:S(2)}) copy-start(bf16[2048,128]{1,0:T(8,128)(2,1)} %copy-done.8) | copy-start | bytes 1572868
  1645.2 299.4 %copy-start.18 = (bf16[384,128]{1,0:T(8,128)(2,1)S(1)}, bf16[384,128]{1,0:T(8,128)(2,1)}, u32[]{:S(2)}) copy-start(bf16[384,128]{1,0:T(8,128)(2,1)} %reduce-scatter.24.cloned.1.call-done) | copy-start | bytes 294916
  1645.2 299.4 %copy-start.22 = (f32[8,1,256]{2,1,0:T(1,128)S(1)}, f32[8,1,256]{2,1,0:T(1,128)}, u32[]{:S(2)}) copy-start(f32[8,1,256]{2,1,0:T(1,128)} %copy-done.21) | copy-start | bytes 24580
  1645.3 299.4 %copy-start.26 = (f32[384]{0:T(512)S(1)}, f32[384]{0:T(512)}, u32[]{:S(2)}) copy-start(f32[384]{0:T(512)} %copy-done.25) | copy-start | bytes 4612
  1833.3 116.6 %copy-start.27 = (bf16[2048]{0:T(1024)(128)(2,1)S(1)}, bf16[2048]{0:T(1024)(128)(2,1)}, u32[]{:S(2)}) copy-start(bf16[2048]{0:T(1024)(128)(2,1)} %get-tuple-element.316) | copy-start | bytes 12292
  1833.3 143.0 %copy-start.28 = (f32[384]{0:T(512)S(1)}, f32[384]{0:T(512)}, u32[]{:S(2)}) copy-start(f32[384]{0:T(512)} %get-tuple-element.400) | copy-start | bytes 4612
  (16 other events, 36.2 us)
Sparse Core Ops, SparseCore 0:
  24.4 115.6 all-gather.11
  142.0 26.1 all-gather.13
  170.1 28.1 all-gather.15
  234.1 211.8 reduce-scatter.13
  447.8 44.3 all-gather.21
  494.1 115.3 all-gather.17
  611.4 41.5 all-gather.19
  654.6 115.3 all-gather.25
  771.8 42.5 all-gather.23
  870.6 211.8 reduce-scatter.17
  1084.8 111.7 reduce-scatter.15
  1203.4 115.8 all-gather.27
  1403.3 18.8 reduce-scatter.21
  1425.0 18.8 reduce-scatter.23
  1447.3 32.4 reduce-scatter.35
  1483.6 34.1 reduce-scatter.37
  1521.1 59.0 reduce-scatter.33
  1583.9 59.0 reduce-scatter.31
  1646.4 59.0 reduce-scatter.29
  1707.8 34.5 all-reduce.6
  1745.6 40.9 reduce-scatter.25
  1790.2 41.2 reduce-scatter.27
  1833.8 110.7 reduce-scatter.19
where the time goes:
time: 2000 us; the launch traced here: 1990 us
  waiting for transfers between devices  1530 us (76%)
  matrix products  286 us (14%)
  other arithmetic  72.1 us (4%)
  blocking collectives  63 us (3%)
  local copies, waits for them, and re-layouts  22.2 us (1%)
    reduce_scatter x1, waiting for transfers between devices, on_device(): lax.psum_scatter(jnp.dot(mixed, out_w, preferred_element_type=jnp.float32...  203 us
    reduce_scatter x1, waiting for transfers between devices, on_device(): lax.psum_scatter(contract_cols(gate_grad, gate_w) + contract_cols(up_grad...  197 us
    all_gather x1, waiting for transfers between devices, on_device(): ffn_normed = lax.all_gather(ffn_own, 'tensor', axis=0, tiled=True)  117 us
    all_gather x1, waiting for transfers between devices, on_device(): lax.all_gather(after_grad.astype(jnp.bfloat16), 'tensor', axis=0, tiled=T...  114 us
    reduce_scatter x1, waiting for transfers between devices, on_device(): lax.psum_scatter(normed_part.astype(jnp.bfloat16), 'tensor', scatter_dime...  111 us
    reduce_scatter x1, waiting for transfers between devices, on_device(): lax.psum_scatter(jnp.dot(hidden, down_w, preferred_element_type=jnp.float...  111 us
    all_gather x1, waiting for transfers between devices, on_device(): grad_full = lax.all_gather(d_out, 'tensor', axis=0, tiled=True)  102 us
    all_gather x1, waiting for transfers between devices, on_device(): normed = lax.all_gather(normed_own, 'tensor', axis=0, tiled=True)  95.1 us
  transfers between devices with their start and end apart: 23, of which 21 were waited for; matrix products, arithmetic and copies ran while one was open for 10% of the time, Pallas kernels for 0%

commit v1 on v0

--- a/solution.py
+++ b/solution.py
@@ -137,7 +137,16 @@
         tiled=True,
     ).astype(jnp.float32)
     output = (after_attn + ffn_part).astype(jnp.bfloat16)
-    grad_full = lax.all_gather(d_out, "tensor", axis=0, tiled=True)
+    devices, here, extent = (lax.axis_size("tensor"), lax.axis_index("tensor"), d_out.shape[0])
+    ahead = [(i, (i + 1) % devices) for i in range(devices)]
+    out = jnp.zeros((*d_out.shape[:0], devices * extent, *d_out.shape[0 + 1 :]), d_out.dtype)
+    block = d_out
+    for hop in range(devices):
+        owner = (here - hop) % devices
+        out = lax.dynamic_update_slice_in_dim(out, block, owner * extent, axis=0)
+        if hop < devices - 1:
+            block = lax.ppermute(block, "tensor", ahead)
+    grad_full = out
     down_grad = contract_rows(hidden, grad_full)
     hidden_grad = contract_cols(grad_full, down_w)
     gate_grad = (hidden_grad * upward * sigma * (1.0 + gate * (1.0 - sigma))).astype(jnp.bfloat16)

time: 2000 us -> 1930 us (0.965)
  waiting for transfers between devices: 1530 us -> 1430 us
  starting transfers between devices: 1.69 us -> 23.3 us
    ppermute x0 -> x3, waiting for transfers between devices: none -> 155 us  [on_device(): block = lax.ppermute(block, 'tensor', ahead)]
    all_gather x1 -> x0, waiting for transfers between devices: 102 us -> none  [on_device(): grad_full = lax.all_gather(d_out, 'tensor', axis=0, tiled=True)]
    all_gather x1, waiting for transfers between devices: 117 us -> 22.4 us  [on_device(): ffn_normed = lax.all_gather(ffn_own, 'tensor', axis=0, tiled=True)]
    all_gather x1, waiting for transfers between devices: 39.5 us -> 0.01 us  [on_device(): lax.all_gather(w_up, 'dp', axis=0, tiled=True)]
    ppermute x0 -> x3, starting transfers between devices: none -> 21.7 us  [on_device(): block = lax.ppermute(block, 'tensor', ahead)]
  transfers between devices with their start and end apart: 23 -> 25, of which waited for: 21 -> 22; matrix products, arithmetic and copies ran while one was open for 10% -> 11% of each run, Pallas kernels for 0% -> 0%
where the time goes in v1:
time: 1930 us
  waiting for transfers between devices  1430 us (74%)
  matrix products  286 us (15%)
  other arithmetic  72 us (4%)
  blocking collectives  63 us (3%)
  local copies, waits for them, and re-layouts  34.8 us (2%)
  starting transfers between devices  23.3 us (1%)
    reduce_scatter x1, waiting for transfers between devices, on_device(): lax.psum_scatter(jnp.dot(mixed, out_w, preferred_element_type=jnp.float32...  202 us
    reduce_scatter x1, waiting for transfers between devices, on_device(): lax.psum_scatter(contract_cols(gate_grad, gate_w) + contract_cols(up_grad...  197 us
    ppermute x3, waiting for transfers between devices, on_device(): block = lax.ppermute(block, 'tensor', ahead)  155 us
    all_gather x1, waiting for transfers between devices, on_device(): lax.all_gather(after_grad.astype(jnp.bfloat16), 'tensor', axis=0, tiled=T...  114 us
    reduce_scatter x1, waiting for transfers between devices, on_device(): lax.psum_scatter(normed_part.astype(jnp.bfloat16), 'tensor', scatter_dime...  111 us
    reduce_scatter x1, waiting for transfers between devices, on_device(): lax.psum_scatter(jnp.dot(hidden, down_w, preferred_element_type=jnp.float...  111 us
    all_gather x1, waiting for transfers between devices, on_device(): normed = lax.all_gather(normed_own, 'tensor', axis=0, tiled=True)  95.1 us
    dot_general x7, matrix products, contract_cols(): lax.dot_general(left, right, (((1,), (1,)), ((), ())), preferred_element_...  77.6 us
  transfers between devices with their start and end apart: 25, of which 22 were waited for; matrix products, arithmetic and copies ran while one was open for 11% of the time, Pallas kernels for 0%

profile of v1, /device:TPU:0, one launch (start us, length us, event | category | flops | bytes accessed | tf_op | source)
XLA Modules:
  0.0 1927.7 jit_solution(1982337292291210324)
XLA Ops:
  10.4 10.3 all-gather
  26.3 9.8 all_gather.39
  36.1 8.9 all_gather.40
  45.0 95.1 %all-gather.11.cloned.1.call-done = bf16[1536,2048]{1,0:T(8,128)(2,1)} async-done(((bf16[384,2048]{1,0:T(8,128)(2,1)}), bf16[1536,2048]{1,0:T(8,128)(2,1)}) %all-gather.11.cloned.1.call-update) | async-done | bytes 6291472 | tf_op jit(solution)/shard_map/all_gather | solution.py:81
  144.9 23.3 %all-gather.13.cloned.1.call-done = bf16[2048,512]{1,0:T(8,128)(2,1)} async-done(((bf16[256,512]{1,0:T(8,128)(2,1)}), bf16[2048,512]{1,0:T(8,128)(2,1)}) %all-gather.13.cloned.1.call-update) | async-done | bytes 2097168 | tf_op jit(solution)/shard_map/all_gather | solution.py:65
  168.2 8.0 convolution_convert_fusion.8
  184.9 40.4 %while.27 = (s32[]{:T(128)}, bf16[3,512,512]{2,1,0:T(8,128)(2,1)S(1)}, f32[3,4,512]{2,1,0:T(4,128)S(1)}, s32[1536]{0:T(1024)S(1)}, s32[3,512]{1,0:T(4,128)S(1)},...) while((s32[]{:T(128)}, ...), condition=%wide.region_6.7_spmd, body=%wide.region_3.6_spmd.sunk | while | flops 1654126592 | bytes 44929176 | solution.py:117
  225.4 8.6 fusion.48
  234.7 8.8 all-gather.1
  243.5 202.5 %reduce-scatter.14.cloned.1.call-done = f32[384,2048]{1,0:T(8,128)} async-done(((f32[1536,2048]{1,0:T(8,128)}), f32[384,2048]{1,0:T(8,128)}) %reduce-scatter.14.cloned.1.call-update) | async-done | bytes 3145744 | tf_op jit(solution)/shard_map/reduce_scatter | solution.py:119
  453.4 36.7 %collective-permute-done = bf16[384,2048]{1,0:T(8,128)(2,1)S(1)} collective-permute-done((bf16[384,2048]{1,0:T(8,128)(2,1)}, bf16[384,2048]{1,0:T(8,128)(2,1)S(1)}, u32[]{:S(2)}, u32[]{:S(2)}) %collective-permute-start) | collective-permute-done | bytes 1572896 | tf_op jit(solution)/shard_map/ppermute | solution.py:148
  491.3 60.1 %collective-permute-done.1 = bf16[384,2048]{1,0:T(8,128)(2,1)} collective-permute-done((bf16[384,2048]{1,0:T(8,128)(2,1)S(1)}, bf16[384,2048]{1,0:T(8,128)(2,1)}, u32[]{:S(2)}, u32[]{:S(2)}) %collective-permute-start.1) | collective-permute-done | bytes 1572896 | tf_op jit(solution)/shard_map/ppermute | solution.py:148
  551.4 20.1 %collective-permute-start.2 = (bf16[384,2048]{1,0:T(8,128)(2,1)}, bf16[384,2048]{1,0:T(8,128)(2,1)}, u32[]{:S(2)}, u32[]{:S(2)}) collective-permute-start(bf16[384,2048]{1,0:T(8,128)(2,1)} %collective-permute-done.1), channel_id=1, source_target_pairs={{0,1},{1,2},{2,3},{3,0},{4,5},{5,6},{6,7},{7,4},{8,9},{9,10},{10,1... | collective-permute-start | bytes 4718600 | tf_op jit(solution)/shard_map/ppermute | solution.py:148
  580.2 58.4 %collective-permute-done.2 = bf16[384,2048]{1,0:T(8,128)(2,1)} collective-permute-done((bf16[384,2048]{1,0:T(8,128)(2,1)}, bf16[384,2048]{1,0:T(8,128)(2,1)}, u32[]{:S(2)}, u32[]{:S(2)}) %collective-permute-start.2) | collective-permute-done | bytes 1572896 | tf_op jit(solution)/shard_map/ppermute | solution.py:148
  641.4 22.4 %all-gather.17.cloned.1.call-done = bf16[1536,2048]{1,0:T(8,128)(2,1)} async-done(((bf16[384,2048]{1,0:T(8,128)(2,1)}), bf16[1536,2048]{1,0:T(8,128)(2,1)}) %all-gather.17.cloned.1.call-update) | async-done | bytes 6291472 | tf_op jit(solution)/shard_map/all_gather | solution.py:128
  663.7 15.3 fusion.50
  679.0 28.2 %all-gather.19.cloned.1.call-done = bf16[2048,1408]{1,0:T(8,128)(2,1)} async-done(((bf16[256,1408]{1,0:T(8,128)(2,1)}), bf16[2048,1408]{1,0:T(8,128)(2,1)}) %all-gather.19.cloned.1.call-update) | async-done | bytes 5767184 | tf_op jit(solution)/shard_map/all_gather | solution.py:72
  707.2 15.1 fusion.49
  722.4 31.1 %all-gather.23.cloned.1.call-done = bf16[1408,2048]{1,0:T(8,128)(2,1)} async-done(((bf16[1408,256]{1,0:T(8,128)(2,1)}), bf16[1408,2048]{1,0:T(8,128)(2,1)}) %all-gather.23.cloned.1.call-update) | async-done | bytes 5767184 | tf_op jit(solution)/shard_map/all_gather | solution.py:74
  753.5 22.9 %multiply_convert_fusion = (bf16[1536,1408]{1,0:T(8,128)(2,1)}, bf16[1536,1408]{1,0:T(8,128)(2,1)}, bf16[1536,1408]{1,0:T(8,128)(2,1)}) fusion(f32[1536,1408]{1,0:T(8,128)} %fusion.49, f32[1536,1408]{1,0:T(8,128)} %fusion.50, bf16[1536,2048]{1,0:T(8,128)(2,1)} %constant_dynamic-update-slice_fusion.2, bf16[1408,2048]{1,0:T(8,128)(2,1)} %all-gather.23.cloned.1.call-done), kind=kOutput, calls=%fused_computation.58 | convolution fusion | flops 8892973056 | bytes 42336256 | tf_op jit(solution)/shard_map/dot_general | solution.py:39
  776.4 16.6 fusion.51
  793.1 16.4 convolution_add_fusion
  809.6 15.0 convolution_convert_fusion.4
  824.7 196.9 %reduce-scatter.18.cloned.1.call-done = f32[384,2048]{1,0:T(8,128)} async-done(((f32[1536,2048]{1,0:T(8,128)}), f32[384,2048]{1,0:T(8,128)}) %reduce-scatter.18.cloned.1.call-update) | async-done | bytes 3145744 | tf_op jit(solution)/shard_map/reduce_scatter | solution.py:156
  1024.8 110.7 %reduce-scatter.16.cloned.1.call-done = bf16[384,2048]{1,0:T(8,128)(2,1)} async-done(((bf16[1536,2048]{1,0:T(8,128)(2,1)}), bf16[384,2048]{1,0:T(8,128)(2,1)}) %reduce-scatter.16.cloned.1.call-update) | async-done | bytes 1572880 | tf_op jit(solution)/shard_map/reduce_scatter | solution.py:133
  1135.5 6.7 fusion.47
  1144.2 114.0 %all-gather.25.cloned.1.call-done = bf16[1536,2048]{1,0:T(8,128)(2,1)} async-done(((bf16[384,2048]{1,0:T(8,128)(2,1)}), bf16[1536,2048]{1,0:T(8,128)(2,1)}) %all-gather.25.cloned.1.call-update) | async-done | bytes 6291472 | tf_op jit(solution)/shard_map/all_gather | solution.py:166
  1258.2 6.9 convolution_convert_fusion.7
  1268.4 71.4 %while.28 = (s32[]{:T(128)}, f32[1536,128]{1,0:T(8,128)}, f32[1536,128]{1,0:T(8,128)S(1)}, bf16[3,512,512]{2,1,0:T(8,128)(2,1)}, s32[1536]{0:T(1024)S(1)}, /*ind...) while((s32[]{:T(128)}, f32[1536,128]{1,0:T(8,128)}, ...), condition=%wide.region_14.15_spmd.clone, body=%wide.region_12.14_spmd.clone.sunk | while | flops 4061853696 | bytes 139145552 | solution.py:210
  1273.7 5.6 fusion.117
  1343.0 17.8 reduce-scatter.22.cloned.1.call-done
  1363.8 18.9 reduce-scatter.24.cloned.1.call-done
  1385.1 14.3 convolution_convert_fusion
  1399.4 15.0 convolution_convert_fusion.1
  1414.8 15.0 convolution_convert_fusion.2
  1429.9 26.8 %reduce-scatter.38.cloned.1.call-done = bf16[256,128]{1,0:T(8,128)(2,1)} async-done(((bf16[2048,128]{1,0:T(8,128)(2,1)}), bf16[256,128]{1,0:T(8,128)(2,1)}) %reduce-scatter.38.cloned.1.call-update) | async-done | bytes 65552 | tf_op jit(solution)/shard_map/reduce_scatter | solution.py:260
  1456.7 7.8 convolution_convert_fusion.6
  1464.6 7.9 convolution_convert_fusion.5
  1472.9 7.2 convolution_convert_fusion.3
  1481.9 37.1 %reduce-scatter.34.cloned.1.call-done = bf16[1408,256]{1,0:T(8,128)(2,1)} async-done(((bf16[1408,2048]{1,0:T(8,128)(2,1)}), bf16[1408,256]{1,0:T(8,128)(2,1)}) %reduce-scatter.34.cloned.1.call-update) | async-done | bytes 720912 | tf_op jit(solution)/shard_map/reduce_scatter | solution.py:275
  1521.4 60.4 %reduce-scatter.32.cloned.1.call-done = bf16[256,1408]{1,0:T(8,128)(2,1)} async-done(((bf16[2048,1408]{1,0:T(8,128)(2,1)}), bf16[256,1408]{1,0:T(8,128)(2,1)}) %reduce-scatter.32.cloned.1.call-update) | async-done | bytes 720912 | tf_op jit(solution)/shard_map/reduce_scatter | solution.py:272
  1584.1 60.1 %reduce-scatter.30.cloned.1.call-done = bf16[256,1408]{1,0:T(8,128)(2,1)} async-done(((bf16[2048,1408]{1,0:T(8,128)(2,1)}), bf16[256,1408]{1,0:T(8,128)(2,1)}) %reduce-scatter.30.cloned.1.call-update) | async-done | bytes 720912 | tf_op jit(solution)/shard_map/reduce_scatter | solution.py:269
  1648.8 32.5 %all-reduce.7.cloned.1.call-done = (bf16[256,128]{1,0:T(8,128)(2,1)}, bf16[256,128]{1,0:T(8,128)(2,1)}) async-done(((bf16[256,128]{1,0:T(8,128)(2,1)}, bf16[256,128]{1,0:T(8,128)(2,1)}), (bf16[256,128]{1,0:T(8,128)(2,1)}, bf16[256,128]{1,0:T(8,128)(2,1)})) %all-reduce.7.cloned.1.call-update) | async-done | bytes 131088 | tf_op jit(solution)/shard_map/psum | solution.py:235
  1684.3 41.1 %reduce-scatter.26.cloned.1.call-done = bf16[256,512]{1,0:T(8,128)(2,1)} async-done(((bf16[2048,512]{1,0:T(8,128)(2,1)}), bf16[256,512]{1,0:T(8,128)(2,1)}) %reduce-scatter.26.cloned.1.call-update) | async-done | bytes 262160 | tf_op jit(solution)/shard_map/reduce_scatter | solution.py:254
  1727.2 43.1 %reduce-scatter.28.cloned.1.call-done = bf16[512,256]{1,0:T(8,128)(2,1)} async-done(((bf16[512,2048]{1,0:T(8,128)(2,1)}), bf16[512,256]{1,0:T(8,128)(2,1)}) %reduce-scatter.28.cloned.1.call-update) | async-done | bytes 262160 | tf_op jit(solution)/shard_map/reduce_scatter | solution.py:263
  1772.1 111.3 %reduce-scatter.20.cloned.1.call-done = bf16[384,2048]{1,0:T(8,128)(2,1)} async-done(((bf16[1536,2048]{1,0:T(8,128)(2,1)}), bf16[384,2048]{1,0:T(8,128)(2,1)}) %reduce-scatter.20.cloned.1.call-update) | async-done | bytes 1572880 | tf_op jit(solution)/shard_map/reduce_scatter | solution.py:217
  1888.7 14.0 all-reduce.2
  1902.8 11.1 all-reduce.3
  (257 shorter events, 195.5 us)
Async XLA Ops:
  7.2 18.7 copy-start.18
  7.2 18.7 copy-start.32
  7.2 19.1 copy-start.19
  7.2 19.1 copy-start.26
  7.2 28.9 %copy-start.27 = (bf16[256,128]{1,0:T(8,128)(2,1)S(1)}, bf16[256,128]{1,0:T(8,128)(2,1)}, u32[]{:S(2)}) copy-start(bf16[256,128]{1,0:T(8,128)(2,1)} %param.24) | copy-start | bytes 196612
  7.2 132.9 %all-gather.11.cloned.1.call-start = ((), (), s32[]{:S(2)}) async-start(), calls=%async_computation.13 | async-start | bytes 7864320 | tf_op jit(solution)/shard_map/all_gather | solution.py:81
  10.4 134.3 %copy-start.28 = (f32[384]{0:T(512)}, f32[384]{0:T(512)S(1)}, u32[]{:S(2)}) copy-start(f32[384]{0:T(512)S(1)} %get-tuple-element.401) | copy-start | bytes 4612
  24.3 143.9 %all-gather.13.cloned.1.call-start = ((), (), s32[]{:S(2)}) async-start(), calls=%async_computation.14 | async-start | bytes 2359296 | tf_op jit(solution)/shard_map/all_gather | solution.py:65
  25.1 200.3 %all-gather.15.cloned.1.call-start = ((), (), s32[]{:S(2)}) async-start(), calls=%async_computation.15 | async-start | bytes 2359296 | tf_op jit(solution)/shard_map/all_gather | solution.py:68
  25.8 420.2 %reduce-scatter.14.cloned.1.call-start = ((), (), s32[]{:S(2)}) async-start(), calls=%async_computation.16 | async-start | bytes 15728640 | tf_op jit(solution)/shard_map/reduce_scatter | solution.py:119
  36.1 144.1 %copy-start.11 = (bf16[2048,128]{1,0:T(8,128)(2,1)}, bf16[2048,128]{1,0:T(8,128)(2,1)S(1)}, u32[]{:S(2)}) copy-start(bf16[2048,128]{1,0:T(8,128)(2,1)S(1)} %all_gather.39) | copy-start | bytes 1572868
  45.0 123.2 %copy-start.9 = (bf16[2048,128]{1,0:T(8,128)(2,1)}, bf16[2048,128]{1,0:T(8,128)(2,1)S(1)}, u32[]{:S(2)}) copy-start(bf16[2048,128]{1,0:T(8,128)(2,1)S(1)} %all_gather.40) | copy-start | bytes 1572868
  144.7 31.4 %copy-start.5 = (bf16[1536,128]{1,0:T(8,128)(2,1)}, bf16[1536,128]{1,0:T(8,128)(2,1)S(1)}, u32[]{:S(2)}) copy-start(bf16[1536,128]{1,0:T(8,128)(2,1)S(1)} %convolution_convert_fusion.11) | copy-start | bytes 1179652
  234.0 407.4 %all-gather.21.cloned.1.call-start = ((), (), s32[]{:S(2)}) async-start(), calls=%async_computation.19 | async-start | bytes 6488064 | tf_op jit(solution)/shard_map/all_gather | solution.py:73
  234.6 429.1 %all-gather.17.cloned.1.call-start = ((), (), s32[]{:S(2)}) async-start(), calls=%async_computation.17 | async-start | bytes 7864320 | tf_op jit(solution)/shard_map/all_gather | solution.py:128
  450.4 256.9 %all-gather.19.cloned.1.call-start = ((), (), s32[]{:S(2)}) async-start(), calls=%async_computation.18 | async-start | bytes 6488064 | tf_op jit(solution)/shard_map/all_gather | solution.py:72
  451.1 302.4 %all-gather.23.cloned.1.call-start = ((), (), s32[]{:S(2)}) async-start(), calls=%async_computation.20 | async-start | bytes 6488064 | tf_op jit(solution)/shard_map/all_gather | solution.py:74
  451.9 569.7 %reduce-scatter.18.cloned.1.call-start = ((), (), s32[]{:S(2)}) async-start(), calls=%async_computation.22 | async-start | bytes 15728640 | tf_op jit(solution)/shard_map/reduce_scatter | solution.py:156
  451.9 38.2 %collective-permute-start = (bf16[384,2048]{1,0:T(8,128)(2,1)}, bf16[384,2048]{1,0:T(8,128)(2,1)S(1)}, u32[]{:S(2)}, u32[]{:S(2)}) collective-permute-start(bf16[384,2048]{1,0:T(8,128)(2,1)} %param.33), channel_id=1, source_target_pairs={{0,1},{1,2},{2,3},{3,0},{4,5},{5,6},{6,7},{7,4},{8,9},{9,10},{10,1... | collective-permute-start | bytes 4718600 | tf_op jit(solution)/shard_map/ppermute | solution.py:148
  491.3 60.1 %collective-permute-start.1 = (bf16[384,2048]{1,0:T(8,128)(2,1)S(1)}, bf16[384,2048]{1,0:T(8,128)(2,1)}, u32[]{:S(2)}, u32[]{:S(2)}) collective-permute-start(bf16[384,2048]{1,0:T(8,128)(2,1)S(1)} %collective-permute-done), channel_id=1, source_target_pairs={{0,1},{1,2},{2,3},{3,0},{4,5},{5,6},{6,7},{7,4},{8,9},{9,10},{10,1... | collective-permute-start | bytes 4718600 | tf_op jit(solution)/shard_map/ppermute | solution.py:148
  551.4 87.3 %collective-permute-start.2 = (bf16[384,2048]{1,0:T(8,128)(2,1)}, bf16[384,2048]{1,0:T(8,128)(2,1)}, u32[]{:S(2)}, u32[]{:S(2)}) collective-permute-start(bf16[384,2048]{1,0:T(8,128)(2,1)} %collective-permute-done.1), channel_id=1, source_target_pairs={{0,1},{1,2},{2,3},{3,0},{4,5},{5,6},{6,7},{7,4},{8,9},{9,10},{10,1... | collective-permute-start | bytes 4718600 | tf_op jit(solution)/shard_map/ppermute | solution.py:148
  776.4 16.6 copy-start.35
  809.5 326.0 %reduce-scatter.16.cloned.1.call-start = ((), (), s32[]{:S(2)}) async-start(), calls=%async_computation.21 | async-start | bytes 7864320 | tf_op jit(solution)/shard_map/reduce_scatter | solution.py:133
  824.6 433.6 %all-gather.25.cloned.1.call-start = ((), (), s32[]{:S(2)}) async-start(), calls=%async_computation.23 | async-start | bytes 7864320 | tf_op jit(solution)/shard_map/all_gather | solution.py:166
  1142.2 218.7 %reduce-scatter.22.cloned.1.call-start = ((), (), s32[]{:S(2)}) async-start(), calls=%async_computation.25 | async-start | bytes 491520 | tf_op jit(solution)/shard_map/reduce_scatter | solution.py:220
  1339.8 42.9 %copy-start.4 = (bf16[384,2048]{1,0:T(8,128)(2,1)S(1)}, bf16[384,2048]{1,0:T(8,128)(2,1)}, u32[]{:S(2)}) copy-start(bf16[384,2048]{1,0:T(8,128)(2,1)} %fusion.39) | copy-start | bytes 4718596
  1339.8 42.9 %copy-start.20 = (bf16[384,128]{1,0:T(8,128)(2,1)S(1)}, bf16[384,128]{1,0:T(8,128)(2,1)}, u32[]{:S(2)}) copy-start(bf16[384,128]{1,0:T(8,128)(2,1)} %param.35) | copy-start | bytes 294916
  1341.9 40.8 %reduce-scatter.24.cloned.1.call-start = ((), (), s32[]{:S(2)}) async-start(), calls=%async_computation.26 | async-start | bytes 491520 | tf_op jit(solution)/shard_map/reduce_scatter | solution.py:223
  1342.8 87.1 %reduce-scatter.36.cloned.1.call-start = ((), (), s32[]{:S(2)}) async-start(), calls=%async_computation.32 | async-start | bytes 589824 | tf_op jit(solution)/shard_map/reduce_scatter | solution.py:257
  1363.8 92.9 %reduce-scatter.38.cloned.1.call-start = ((), (), s32[]{:S(2)}) async-start(), calls=%async_computation.33 | async-start | bytes 589824 | tf_op jit(solution)/shard_map/reduce_scatter | solution.py:260
  1385.0 134.0 %reduce-scatter.34.cloned.1.call-start = ((), (), s32[]{:S(2)}) async-start(), calls=%async_computation.31 | async-start | bytes 6488064 | tf_op jit(solution)/shard_map/reduce_scatter | solution.py:275
  1399.4 182.4 %reduce-scatter.32.cloned.1.call-start = ((), (), s32[]{:S(2)}) async-start(), calls=%async_computation.30 | async-start | bytes 6488064 | tf_op jit(solution)/shard_map/reduce_scatter | solution.py:272
  1414.5 229.7 %reduce-scatter.30.cloned.1.call-start = ((), (), s32[]{:S(2)}) async-start(), calls=%async_computation.29 | async-start | bytes 6488064 | tf_op jit(solution)/shard_map/reduce_scatter | solution.py:269
  1429.8 26.9 %copy-start.13 = (bf16[3,512,512]{2,1,0:T(8,128)(2,1)S(1)}, bf16[3,512,512]{2,1,0:T(8,128)(2,1)}, u32[]{:S(2)}) copy-start(bf16[3,512,512]{2,1,0:T(8,128)(2,1)} %get-tuple-element.157) | copy-start | bytes 4718596
  1429.8 251.5 %all-reduce.7.cloned.1.call-start = ((), (), s32[]{:S(2)}) async-start(), calls=%async_computation.34 | async-start | bytes 262144 | tf_op jit(solution)/shard_map/psum | solution.py:235
  1456.7 268.7 %reduce-scatter.26.cloned.1.call-start = ((), (), s32[]{:S(2)}) async-start(), calls=%async_computation.27 | async-start | bytes 2359296 | tf_op jit(solution)/shard_map/reduce_scatter | solution.py:254
  1464.5 305.8 %reduce-scatter.28.cloned.1.call-start = ((), (), s32[]{:S(2)}) async-start(), calls=%async_computation.28 | async-start | bytes 2359296 | tf_op jit(solution)/shard_map/reduce_scatter | solution.py:263
  1472.5 410.8 %reduce-scatter.20.cloned.1.call-start = ((), (), s32[]{:S(2)}) async-start(), calls=%async_computation.24 | async-start | bytes 7864320 | tf_op jit(solution)/shard_map/reduce_scatter | solution.py:217
  1480.0 166.4 %copy-start.12 = (bf16[2048,128]{1,0:T(8,128)(2,1)S(1)}, bf16[2048,128]{1,0:T(8,128)(2,1)}, u32[]{:S(2)}) copy-start(bf16[2048,128]{1,0:T(8,128)(2,1)} %copy-done.11) | copy-start | bytes 1572868
  1480.1 166.4 %copy-start.22 = (bf16[384,128]{1,0:T(8,128)(2,1)S(1)}, bf16[384,128]{1,0:T(8,128)(2,1)}, u32[]{:S(2)}) copy-start(bf16[384,128]{1,0:T(8,128)(2,1)} %param.34) | copy-start | bytes 294916
  1480.1 166.4 %copy-start.23 = (bf16[384,128]{1,0:T(8,128)(2,1)S(1)}, bf16[384,128]{1,0:T(8,128)(2,1)}, u32[]{:S(2)}) copy-start(bf16[384,128]{1,0:T(8,128)(2,1)} %reduce-scatter.22.cloned.1.call-done) | copy-start | bytes 294916
  1584.1 299.3 %copy-start.1 = (bf16[384,2048]{1,0:T(8,128)(2,1)S(1)}, bf16[384,2048]{1,0:T(8,128)(2,1)}, u32[]{:S(2)}) copy-start(bf16[384,2048]{1,0:T(8,128)(2,1)} %param.20) | copy-start | bytes 4718596
  1584.1 299.3 %copy-start.10 = (bf16[2048,128]{1,0:T(8,128)(2,1)S(1)}, bf16[2048,128]{1,0:T(8,128)(2,1)}, u32[]{:S(2)}) copy-start(bf16[2048,128]{1,0:T(8,128)(2,1)} %copy-done.9) | copy-start | bytes 1572868
  1584.1 299.3 %copy-start.21 = (bf16[384,128]{1,0:T(8,128)(2,1)S(1)}, bf16[384,128]{1,0:T(8,128)(2,1)}, u32[]{:S(2)}) copy-start(bf16[384,128]{1,0:T(8,128)(2,1)} %reduce-scatter.24.cloned.1.call-done) | copy-start | bytes 294916
  1584.1 299.3 %copy-start.25 = (f32[8,1,256]{2,1,0:T(1,128)S(1)}, f32[8,1,256]{2,1,0:T(1,128)}, u32[]{:S(2)}) copy-start(f32[8,1,256]{2,1,0:T(1,128)} %copy-done.24) | copy-start | bytes 24580
  1584.1 299.3 %copy-start.29 = (f32[384]{0:T(512)S(1)}, f32[384]{0:T(512)}, u32[]{:S(2)}) copy-start(f32[384]{0:T(512)} %copy-done.28) | copy-start | bytes 4612
  1772.1 116.6 %copy-start.30 = (bf16[2048]{0:T(1024)(128)(2,1)S(1)}, bf16[2048]{0:T(1024)(128)(2,1)}, u32[]{:S(2)}) copy-start(bf16[2048]{0:T(1024)(128)(2,1)} %get-tuple-element.316) | copy-start | bytes 12292
  1772.1 143.0 %copy-start.31 = (f32[384]{0:T(512)S(1)}, f32[384]{0:T(512)}, u32[]{:S(2)}) copy-start(f32[384]{0:T(512)} %get-tuple-element.400) | copy-start | bytes 4612
  (21 other events, 62.8 us)
Sparse Core Ops, SparseCore 0:
  24.4 115.6 all-gather.10
  142.0 26.1 all-gather.12
  170.0 28.1 all-gather.14
  234.1 211.8 reduce-scatter.13
  447.7 44.3 all-gather.20
  494.1 169.5 all-gather.16
  665.6 41.5 all-gather.18
  709.1 44.3 all-gather.22
  809.6 211.8 reduce-scatter.17
  1023.7 111.7 reduce-scatter.15
  1142.3 115.8 all-gather.24
  1342.0 18.7 reduce-scatter.21
  1363.8 18.8 reduce-scatter.23
  1386.2 32.3 reduce-scatter.35
  1422.4 34.1 reduce-scatter.37
  1459.9 59.0 reduce-scatter.33
  1522.7 59.0 reduce-scatter.31
  1585.1 59.0 reduce-scatter.29
  1646.7 34.5 all-reduce.6
  1684.4 40.9 reduce-scatter.25
  1729.0 41.2 reduce-scatter.27
  1772.6 110.7 reduce-scatter.19
